TPU v7x, 512 devices: a whole 4x4x16 slice. The times are simulated.
512 devices in a mesh: ev: 8 (over y_hi, x), sp: 64 (over z, y_lo, core).
Axes of the slice: x: 4, y: 4 (y_hi: 2, y_lo: 2; y = y_hi * 2 + y_lo), z: 16, core: 2. Of those that a mesh axis runs over, the one named last changes fastest.
Arguments:
- partial_kernels: float32 [8, 32, 512, 128], P('ev', None, 'sp'), may hold values from -6 to 6
- block_ids: int32 [8, 512], P('ev', 'sp'), may hold values from 0 to 255, as said below
- radial_smoother: float32 [128, 128], replicated, may hold values from -0.5 to 2
- shell_level: int32 [128], P('sp'), may hold values from 1 to 4
- lateral_scale: float32 [512, 1024], replicated, may hold values from 0.5 to 1
Outputs:
- smoothed_kernel: float32 [128, 512, 1024], P('sp', None, 'ev')
Inputs may be any that keep to these rules, and one draw needn't show every extreme that they name: `block_ids`: each index of ev and sp holds 8 distinct ids; an id's owner is id // 32; one holder gives at most 2 ids to one owner, and in every stripe some owner receives 2 ids from every group.
All inputs are finite; a program needn't handle non-finite values.
Results may differ from a plain program's by a relative error of at most 0.000073.
Values sent between devices are 32-bit elements; how exact they have to be, the bound alone decides.
No kernel may reach another device: no remote copies, remote signals or barrier semaphores. Data moves between devices by JAX's collectives and lax.ppermute only.
A program may use at most 64 MiB of HBM per device.

v0:
```python
import jax
import jax.numpy as jnp
from jax import lax
from jax.sharding import PartitionSpec as P

NR = 128
BPT = 8
CAP = 2
PASSES = 4
NSEG = 4
diffusion_rate = 0.0615


def padded_2(cells, sides, width):
    for axis, dim in sides:
        count = lax.axis_size(axis)
        ends = count - 1
        head = lax.slice_in_dim(cells, 0, width, axis=dim)
        tail = lax.slice_in_dim(cells, cells.shape[dim] - width, cells.shape[dim], axis=dim)
        cells = jnp.concatenate(
            [
                lax.ppermute(tail, axis, [(i, (i + 1) % count) for i in range(ends)]),
                cells,
                lax.ppermute(head, axis, [((i + 1) % count, i) for i in range(ends)]),
            ],
            axis=dim,
        )
    return cells


def per_device(partial_kernels, block_ids, radial_smoother, shell_level, lateral_scale):
    groups = lax.axis_size("ev")
    per_owner = BPT * NSEG
    blocks = partial_kernels[0]
    block_list = block_ids[0]
    owners = block_list // per_owner
    within = block_list % per_owner
    listed = block_list.shape[0]
    same_owner = owners[:, None] == owners[None, :]
    earlier = jnp.arange(listed)[None, :] < jnp.arange(listed)[:, None]
    ranking = jnp.sum(same_owner & earlier, axis=1)
    slot_of = owners * CAP + ranking
    placing = (slot_of[None, :] == jnp.arange(groups * CAP, dtype=jnp.int32)[:, None]).astype(
        jnp.float32
    )
    packed = jnp.einsum("rjc,sj->rsc", blocks, placing, precision=lax.Precision.HIGHEST)
    label_out = (
        jnp.dot(placing, within.astype(jnp.float32) + 1.0, precision=lax.Precision.HIGHEST) - 1.0
    )
    label_out = label_out.reshape(1, groups * CAP, 1)
    arrived, labels = (
        lax.all_to_all(packed, "ev", split_axis=1, concat_axis=1, tiled=True),
        lax.all_to_all(label_out, "ev", split_axis=1, concat_axis=1, tiled=True),
    )
    picker = (labels.reshape(1, -1) == jnp.arange(per_owner, dtype=jnp.float32)[:, None]).astype(
        jnp.float32
    )
    column_tile = jnp.einsum("rsc,ls->lrc", arrived, picker, precision=lax.Precision.HIGHEST)
    tile_width = column_tile.shape[2]
    columns = column_tile.reshape(BPT, NR, tile_width)
    smoothed = jnp.einsum("rq,kqc->rkc", radial_smoother, columns, precision=lax.Precision.HIGHEST)
    shells = lax.all_to_all(smoothed, "sp", split_axis=0, concat_axis=1, tiled=True)
    ev_index = lax.axis_index("ev")
    levels = shell_level.astype(jnp.float32)[:, None, None]
    scale_here = lax.dynamic_slice_in_dim(lateral_scale, ev_index * tile_width, tile_width, 1)
    coefficient = diffusion_rate * levels * scale_here[None]
    kernel_field = shells
    for repeat in range(PASSES):
        padded = padded_2(kernel_field, (("ev", 2),), 1)
        padded = jnp.pad(padded, ((0, 0), (1, 1), (0, 0)))
        beside = (
            padded[:, 2:, 1:-1] + padded[:, :-2, 1:-1] + padded[:, 1:-1, 2:] + padded[:, 1:-1, :-2]
        )
        kernel_field = kernel_field + coefficient * (beside - 4.0 * kernel_field)
    return kernel_field


def solution(mesh):
    placed = (P("ev", None, "sp", None), P("ev", "sp"), P(), P("sp"), P())
    return jax.shard_map(
        per_device, mesh=mesh, in_specs=placed, out_specs=P("sp", None, "ev"), check_vma=False
    )
```

profile of v0, /device:TPU:88, one launch (start us, length us, event | category | flops | bytes accessed | tf_op | source)
XLA Modules:
  0.0 168.2 jit_solution(15304359649547561368)
XLA Ops:
  0.0 0.8 fusion.47
  2.3 0.8 fusion.1
  3.9 7.3 %all-to-all-start = ((f32[1,16,1]{2,0,1:T(1,128)}), f32[1,16,1]{2,0,1:T(1,128)S(1)}, u32[]{:S(2)}, u32[]{:S(2)}) async-start(f32[1,16,1]{2,0,1:T(1,128)} %copy.28), calls=%async_computation | async-start | bytes 16384 | tf_op jit(solution)/shard_map/all_to_all | solution.py:53
  11.1 1.3 convolution_bitcast_fusion.1
  12.4 0.8 copy.29
  13.2 2.7 %all-to-all-done = f32[1,16,1]{2,0,1:T(1,128)S(1)} async-done(((f32[1,16,1]{2,0,1:T(1,128)}), f32[1,16,1]{2,0,1:T(1,128)S(1)}, u32[]{:S(2)}, u32[]{:S(2)}) %all-to-all-start) | async-done | bytes 96 | tf_op jit(solution)/shard_map/all_to_all | solution.py:53
  15.8 6.3 %all-to-all-start.1 = ((f32[32,16,128]{2,0,1:T(8,128)}), f32[32,16,128]{2,0,1:T(8,128)S(1)}, u32[]{:S(2)}, u32[]{:S(2)}) async-start(f32[32,16,128]{2,0,1:T(8,128)} %copy.29), calls=%async_computation.1 | async-start | bytes 524288 | tf_op jit(solution)/shard_map/all_to_all | solution.py:52
  22.4 5.6 %all-to-all-done.1 = f32[32,16,128]{2,0,1:T(8,128)S(1)} async-done(((f32[32,16,128]{2,0,1:T(8,128)}), f32[32,16,128]{2,0,1:T(8,128)S(1)}, u32[]{:S(2)}, u32[]{:S(2)}) %all-to-all-start.1) | async-done | bytes 262176 | tf_op jit(solution)/shard_map/all_to_all | solution.py:52
  28.9 1.0 convolution_bitcast_fusion
  29.9 1.0 copy.33
  30.9 16.2 %all-to-all-start.2 = ((f32[128,8,128]{2,1,0:T(8,128)}), f32[128,8,128]{2,1,0:T(8,128)S(1)}, u32[]{:S(2)}, u32[]{:S(2)}) async-start(f32[128,8,128]{2,1,0:T(8,128)} %copy.33), calls=%async_computation.2 | async-start | bytes 1048576 | tf_op jit(solution)/shard_map/all_to_all | solution.py:62
  47.1 29.4 %all-to-all-done.2 = f32[128,8,128]{2,1,0:T(8,128)S(1)} async-done(((f32[128,8,128]{2,1,0:T(8,128)}), f32[128,8,128]{2,1,0:T(8,128)S(1)}, u32[]{:S(2)}, u32[]{:S(2)}) %all-to-all-start.2) | async-done | bytes 524320 | tf_op jit(solution)/shard_map/all_to_all | solution.py:62
  76.7 5.4 %collective-permute-start.1 = (f32[2,512,1]{2,1,0:T(8,128)S(1)}, f32[2,512,1]{2,1,0:T(8,128)S(1)}, u32[]{:S(2)}, u32[]{:S(2)}) collective-permute-start(f32[2,512,1]{2,1,0:T(8,128)S(1)} %get-tuple-element.11), channel_id=1, source_target_pairs={{64,0},{128,64},{192,128},{256,192},{320,256},{384,320},{448,384},... | collective-permute-start | bytes 12296 | tf_op jit(solution)/shard_map/ppermute | solution.py:24
  82.1 1.9 %collective-permute-start = (f32[2,512,1]{2,1,0:T(8,128)S(1)}, f32[2,512,1]{2,1,0:T(8,128)S(1)}, u32[]{:S(2)}, u32[]{:S(2)}) collective-permute-start(f32[2,512,1]{2,1,0:T(8,128)S(1)} %get-tuple-element.12), channel_id=1, source_target_pairs={{0,64},{64,128},{128,192},{192,256},{256,320},{320,384},{384,448},... | collective-permute-start | bytes 12296 | tf_op jit(solution)/shard_map/ppermute | solution.py:22
  84.1 10.0 %collective-permute-done.1 = f32[2,512,1]{2,1,0:T(8,128)S(1)} collective-permute-done((f32[2,512,1]{2,1,0:T(8,128)S(1)}, f32[2,512,1]{2,1,0:T(8,128)S(1)}, u32[]{:S(2)}, u32[]{:S(2)}) %collective-permute-start.1) | collective-permute-done | bytes 4128 | tf_op jit(solution)/shard_map/ppermute | solution.py:24
  94.1 7.7 %collective-permute-done = f32[2,512,1]{2,1,0:T(8,128)S(1)} collective-permute-done((f32[2,512,1]{2,1,0:T(8,128)S(1)}, f32[2,512,1]{2,1,0:T(8,128)S(1)}, u32[]{:S(2)}, u32[]{:S(2)}) %collective-permute-start) | collective-permute-done | bytes 4128 | tf_op jit(solution)/shard_map/ppermute | solution.py:22
  102.4 0.8 fusion.3
  103.3 1.9 %collective-permute-start.3 = (f32[2,512,1]{2,1,0:T(8,128)S(1)}, f32[2,512,1]{2,1,0:T(8,128)S(1)}, u32[]{:S(2)}, u32[]{:S(2)}) collective-permute-start(f32[2,512,1]{2,1,0:T(8,128)S(1)} %get-tuple-element.9), channel_id=1, source_target_pairs={{64,0},{128,64},{192,128},{256,192},{320,256},{384,320},{448,384},... | collective-permute-start | bytes 12296 | tf_op jit(solution)/shard_map/ppermute | solution.py:24
  105.3 3.9 %collective-permute-start.2 = (f32[2,512,1]{2,1,0:T(8,128)S(1)}, f32[2,512,1]{2,1,0:T(8,128)S(1)}, u32[]{:S(2)}, u32[]{:S(2)}) collective-permute-start(f32[2,512,1]{2,1,0:T(8,128)S(1)} %get-tuple-element.10), channel_id=1, source_target_pairs={{0,64},{64,128},{128,192},{192,256},{256,320},{320,384},{384,448},... | collective-permute-start | bytes 12296 | tf_op jit(solution)/shard_map/ppermute | solution.py:22
  109.2 9.4 %collective-permute-done.3 = f32[2,512,1]{2,1,0:T(8,128)S(1)} collective-permute-done((f32[2,512,1]{2,1,0:T(8,128)S(1)}, f32[2,512,1]{2,1,0:T(8,128)S(1)}, u32[]{:S(2)}, u32[]{:S(2)}) %collective-permute-start.3) | collective-permute-done | bytes 4128 | tf_op jit(solution)/shard_map/ppermute | solution.py:24
  118.6 5.5 %collective-permute-done.2 = f32[2,512,1]{2,1,0:T(8,128)S(1)} collective-permute-done((f32[2,512,1]{2,1,0:T(8,128)S(1)}, f32[2,512,1]{2,1,0:T(8,128)S(1)}, u32[]{:S(2)}, u32[]{:S(2)}) %collective-permute-start.2) | collective-permute-done | bytes 4128 | tf_op jit(solution)/shard_map/ppermute | solution.py:22
  124.6 0.8 fusion.4
  125.6 1.9 %collective-permute-start.5 = (f32[2,512,1]{2,1,0:T(8,128)S(1)}, f32[2,512,1]{2,1,0:T(8,128)S(1)}, u32[]{:S(2)}, u32[]{:S(2)}) collective-permute-start(f32[2,512,1]{2,1,0:T(8,128)S(1)} %get-tuple-element.7), channel_id=1, source_target_pairs={{64,0},{128,64},{192,128},{256,192},{320,256},{384,320},{448,384},... | collective-permute-start | bytes 12296 | tf_op jit(solution)/shard_map/ppermute | solution.py:24
  127.6 3.9 %collective-permute-start.4 = (f32[2,512,1]{2,1,0:T(8,128)S(1)}, f32[2,512,1]{2,1,0:T(8,128)S(1)}, u32[]{:S(2)}, u32[]{:S(2)}) collective-permute-start(f32[2,512,1]{2,1,0:T(8,128)S(1)} %get-tuple-element.8), channel_id=1, source_target_pairs={{0,64},{64,128},{128,192},{192,256},{256,320},{320,384},{384,448},... | collective-permute-start | bytes 12296 | tf_op jit(solution)/shard_map/ppermute | solution.py:22
  131.5 8.6 %collective-permute-done.5 = f32[2,512,1]{2,1,0:T(8,128)S(1)} collective-permute-done((f32[2,512,1]{2,1,0:T(8,128)S(1)}, f32[2,512,1]{2,1,0:T(8,128)S(1)}, u32[]{:S(2)}, u32[]{:S(2)}) %collective-permute-start.5) | collective-permute-done | bytes 4128 | tf_op jit(solution)/shard_map/ppermute | solution.py:24
  140.0 5.5 %collective-permute-done.4 = f32[2,512,1]{2,1,0:T(8,128)S(1)} collective-permute-done((f32[2,512,1]{2,1,0:T(8,128)S(1)}, f32[2,512,1]{2,1,0:T(8,128)S(1)}, u32[]{:S(2)}, u32[]{:S(2)}) %collective-permute-start.4) | collective-permute-done | bytes 4128 | tf_op jit(solution)/shard_map/ppermute | solution.py:22
  146.1 0.8 fusion.5
  147.1 1.9 %collective-permute-start.7 = (f32[2,512,1]{2,1,0:T(8,128)S(1)}, f32[2,512,1]{2,1,0:T(8,128)S(1)}, u32[]{:S(2)}, u32[]{:S(2)}) collective-permute-start(f32[2,512,1]{2,1,0:T(8,128)S(1)} %get-tuple-element.5), channel_id=1, source_target_pairs={{64,0},{128,64},{192,128},{256,192},{320,256},{384,320},{448,384},... | collective-permute-start | bytes 12296 | tf_op jit(solution)/shard_map/ppermute | solution.py:24
  149.0 3.9 %collective-permute-start.6 = (f32[2,512,1]{2,1,0:T(8,128)S(1)}, f32[2,512,1]{2,1,0:T(8,128)S(1)}, u32[]{:S(2)}, u32[]{:S(2)}) collective-permute-start(f32[2,512,1]{2,1,0:T(8,128)S(1)} %get-tuple-element.6), channel_id=1, source_target_pairs={{0,64},{64,128},{128,192},{192,256},{256,320},{320,384},{384,448},... | collective-permute-start | bytes 12296 | tf_op jit(solution)/shard_map/ppermute | solution.py:22
  152.9 7.7 %collective-permute-done.7 = f32[2,512,1]{2,1,0:T(8,128)S(1)} collective-permute-done((f32[2,512,1]{2,1,0:T(8,128)S(1)}, f32[2,512,1]{2,1,0:T(8,128)S(1)}, u32[]{:S(2)}, u32[]{:S(2)}) %collective-permute-start.7) | collective-permute-done | bytes 4128 | tf_op jit(solution)/shard_map/ppermute | solution.py:24
  160.6 5.5 %collective-permute-done.6 = f32[2,512,1]{2,1,0:T(8,128)S(1)} collective-permute-done((f32[2,512,1]{2,1,0:T(8,128)S(1)}, f32[2,512,1]{2,1,0:T(8,128)S(1)}, u32[]{:S(2)}, u32[]{:S(2)}) %collective-permute-start.6) | collective-permute-done | bytes 4128 | tf_op jit(solution)/shard_map/ppermute | solution.py:22
  166.6 1.5 fusion.6
  (24 shorter events, 6.1 us)
Async XLA Ops:
  0.0 84.1 %copy-start = (f32[512,1024]{1,0:T(8,128)S(1)}, f32[512,1024]{1,0:T(8,128)}, u32[]{:S(2)}) copy-start(f32[512,1024]{1,0:T(8,128)} %param.9) | copy-start | bytes 6291460
  3.9 12.0 %all-to-all-start = ((f32[1,16,1]{2,0,1:T(1,128)}), f32[1,16,1]{2,0,1:T(1,128)S(1)}, u32[]{:S(2)}, u32[]{:S(2)}) async-start(f32[1,16,1]{2,0,1:T(1,128)} %copy.28), calls=%async_computation | async-start | bytes 16384 | tf_op jit(solution)/shard_map/all_to_all | solution.py:53
  13.2 15.7 %copy-start.1 = (f32[128,128]{1,0:T(8,128)S(1)}, f32[128,128]{1,0:T(8,128)}, u32[]{:S(2)}) copy-start(f32[128,128]{1,0:T(8,128)} %param.7) | copy-start | bytes 196612
  15.8 12.1 %all-to-all-start.1 = ((f32[32,16,128]{2,0,1:T(8,128)}), f32[32,16,128]{2,0,1:T(8,128)S(1)}, u32[]{:S(2)}, u32[]{:S(2)}) async-start(f32[32,16,128]{2,0,1:T(8,128)} %copy.29), calls=%async_computation.1 | async-start | bytes 524288 | tf_op jit(solution)/shard_map/all_to_all | solution.py:52
  29.9 17.2 %copy-start.2 = (s32[2]{0:T(128)S(1)}, s32[2]{0:T(128)}, u32[]{:S(2)}) copy-start(s32[2]{0:T(128)} %param.8) | copy-start | bytes 28
  30.9 45.6 %all-to-all-start.2 = ((f32[128,8,128]{2,1,0:T(8,128)}), f32[128,8,128]{2,1,0:T(8,128)S(1)}, u32[]{:S(2)}, u32[]{:S(2)}) async-start(f32[128,8,128]{2,1,0:T(8,128)} %copy.33), calls=%async_computation.2 | async-start | bytes 1048576 | tf_op jit(solution)/shard_map/all_to_all | solution.py:62
  76.7 17.4 %collective-permute-start.1 = (f32[2,512,1]{2,1,0:T(8,128)S(1)}, f32[2,512,1]{2,1,0:T(8,128)S(1)}, u32[]{:S(2)}, u32[]{:S(2)}) collective-permute-start(f32[2,512,1]{2,1,0:T(8,128)S(1)} %get-tuple-element.11), channel_id=1, source_target_pairs={{64,0},{128,64},{192,128},{256,192},{320,256},{384,320},{448,384},... | collective-permute-start | bytes 12296 | tf_op jit(solution)/shard_map/ppermute | solution.py:24
  82.1 19.7 %collective-permute-start = (f32[2,512,1]{2,1,0:T(8,128)S(1)}, f32[2,512,1]{2,1,0:T(8,128)S(1)}, u32[]{:S(2)}, u32[]{:S(2)}) collective-permute-start(f32[2,512,1]{2,1,0:T(8,128)S(1)} %get-tuple-element.12), channel_id=1, source_target_pairs={{0,64},{64,128},{128,192},{192,256},{256,320},{320,384},{384,448},... | collective-permute-start | bytes 12296 | tf_op jit(solution)/shard_map/ppermute | solution.py:22
  103.3 15.3 %collective-permute-start.3 = (f32[2,512,1]{2,1,0:T(8,128)S(1)}, f32[2,512,1]{2,1,0:T(8,128)S(1)}, u32[]{:S(2)}, u32[]{:S(2)}) collective-permute-start(f32[2,512,1]{2,1,0:T(8,128)S(1)} %get-tuple-element.9), channel_id=1, source_target_pairs={{64,0},{128,64},{192,128},{256,192},{320,256},{384,320},{448,384},... | collective-permute-start | bytes 12296 | tf_op jit(solution)/shard_map/ppermute | solution.py:24
  105.3 18.9 %collective-permute-start.2 = (f32[2,512,1]{2,1,0:T(8,128)S(1)}, f32[2,512,1]{2,1,0:T(8,128)S(1)}, u32[]{:S(2)}, u32[]{:S(2)}) collective-permute-start(f32[2,512,1]{2,1,0:T(8,128)S(1)} %get-tuple-element.10), channel_id=1, source_target_pairs={{0,64},{64,128},{128,192},{192,256},{256,320},{320,384},{384,448},... | collective-permute-start | bytes 12296 | tf_op jit(solution)/shard_map/ppermute | solution.py:22
  125.6 14.4 %collective-permute-start.5 = (f32[2,512,1]{2,1,0:T(8,128)S(1)}, f32[2,512,1]{2,1,0:T(8,128)S(1)}, u32[]{:S(2)}, u32[]{:S(2)}) collective-permute-start(f32[2,512,1]{2,1,0:T(8,128)S(1)} %get-tuple-element.7), channel_id=1, source_target_pairs={{64,0},{128,64},{192,128},{256,192},{320,256},{384,320},{448,384},... | collective-permute-start | bytes 12296 | tf_op jit(solution)/shard_map/ppermute | solution.py:24
  127.6 18.0 %collective-permute-start.4 = (f32[2,512,1]{2,1,0:T(8,128)S(1)}, f32[2,512,1]{2,1,0:T(8,128)S(1)}, u32[]{:S(2)}, u32[]{:S(2)}) collective-permute-start(f32[2,512,1]{2,1,0:T(8,128)S(1)} %get-tuple-element.8), channel_id=1, source_target_pairs={{0,64},{64,128},{128,192},{192,256},{256,320},{320,384},{384,448},... | collective-permute-start | bytes 12296 | tf_op jit(solution)/shard_map/ppermute | solution.py:22
  147.1 13.6 %collective-permute-start.7 = (f32[2,512,1]{2,1,0:T(8,128)S(1)}, f32[2,512,1]{2,1,0:T(8,128)S(1)}, u32[]{:S(2)}, u32[]{:S(2)}) collective-permute-start(f32[2,512,1]{2,1,0:T(8,128)S(1)} %get-tuple-element.5), channel_id=1, source_target_pairs={{64,0},{128,64},{192,128},{256,192},{320,256},{384,320},{448,384},... | collective-permute-start | bytes 12296 | tf_op jit(solution)/shard_map/ppermute | solution.py:24
  149.0 17.2 %collective-permute-start.6 = (f32[2,512,1]{2,1,0:T(8,128)S(1)}, f32[2,512,1]{2,1,0:T(8,128)S(1)}, u32[]{:S(2)}, u32[]{:S(2)}) collective-permute-start(f32[2,512,1]{2,1,0:T(8,128)S(1)} %get-tuple-element.6), channel_id=1, source_target_pairs={{0,64},{64,128},{128,192},{192,256},{256,320},{320,384},{384,448},... | collective-permute-start | bytes 12296 | tf_op jit(solution)/shard_map/ppermute | solution.py:22
where the time goes:
time: 169 us; the launch traced here: 168 us
  waiting for transfers between devices  97.7 us (58%)
  starting transfers between devices  54.6 us (32%)
  other arithmetic  8.32 us (5%)
  local copies, waits for them, and re-layouts  3.67 us (2%)
  matrix products  3.66 us (2%)
    ppermute x4, waiting for transfers between devices, padded_2(): lax.ppermute(head, axis, [((i + 1) % count, i) for i in range(ends)])  35.7 us
    all_to_all x1, waiting for transfers between devices, per_device(): lax.all_to_all(smoothed, 'sp', split_axis=0, concat_axis=1, tiled=True)  29.4 us
    ppermute x4, waiting for transfers between devices, padded_2(): lax.ppermute(tail, axis, [(i, (i + 1) % count) for i in range(ends)])  24.4 us
    all_to_all x1, starting transfers between devices, per_device(): lax.all_to_all(smoothed, 'sp', split_axis=0, concat_axis=1, tiled=True)  16.2 us
    ppermute x4, starting transfers between devices, padded_2(): lax.ppermute(tail, axis, [(i, (i + 1) % count) for i in range(ends)])  13.7 us
    ppermute x4, starting transfers between devices, padded_2(): lax.ppermute(head, axis, [((i + 1) % count, i) for i in range(ends)])  11.2 us
    all_to_all x1, starting transfers between devices, per_device(): lax.all_to_all(label_out, 'ev', split_axis=1, concat_axis=1, tiled=True)  7.26 us
    all_to_all x1, starting transfers between devices, per_device(): lax.all_to_all(packed, 'ev', split_axis=1, concat_axis=1, tiled=True)  6.3 us
  transfers between devices with their start and end apart: 11, of which 11 were waited for; matrix products, arithmetic and copies ran while one was open for 1% of the time, Pallas kernels for 0%

commit v1 on v0

--- a/solution.py
+++ b/solution.py
@@ -50,7 +50,12 @@
     label_out = label_out.reshape(1, groups * CAP, 1)
     arrived, labels = (
         lax.all_to_all(packed, "ev", split_axis=1, concat_axis=1, tiled=True),
-        lax.all_to_all(label_out, "ev", split_axis=1, concat_axis=1, tiled=True),
+        jnp.concatenate(
+            lax.all_to_all(
+                jnp.stack(jnp.split(label_out, lax.axis_size("ev"), axis=1)), "ev", 0, 0
+            ),
+            axis=1,
+        ),
     )
     picker = (labels.reshape(1, -1) == jnp.arange(per_owner, dtype=jnp.float32)[:, None]).astype(
         jnp.float32

time: 169 us -> 173 us (1.024)
  local copies, waits for them, and re-layouts: 3.67 us -> 8.48 us
    unnamed x6 -> x13, local copies, waits for them, and re-layouts: 0.01 us -> 4.27 us
  transfers between devices with their start and end apart: 11 -> 11, of which waited for: 11 -> 11; matrix products, arithmetic and copies ran while one was open for 1% -> 2% of each run, Pallas kernels for 0% -> 0%
where the time goes in v1:
time: 173 us; the launch traced here: 172 us
  waiting for transfers between devices  96.6 us (56%)
  starting transfers between devices  54.6 us (32%)
  other arithmetic  8.75 us (5%)
  local copies, waits for them, and re-layouts  8.48 us (5%)
  matrix products  3.66 us (2%)
    ppermute x4, waiting for transfers between devices, padded_2(): lax.ppermute(head, axis, [((i + 1) % count, i) for i in range(ends)])  35.7 us
    all_to_all x1, waiting for transfers between devices, per_device(): lax.all_to_all(smoothed, 'sp', split_axis=0, concat_axis=1, tiled=True)  29.4 us
    ppermute x4, waiting for transfers between devices, padded_2(): lax.ppermute(tail, axis, [(i, (i + 1) % count) for i in range(ends)])  24.4 us
    all_to_all x1, starting transfers between devices, per_device(): lax.all_to_all(smoothed, 'sp', split_axis=0, concat_axis=1, tiled=True)  16.2 us
    ppermute x4, starting transfers between devices, padded_2(): lax.ppermute(tail, axis, [(i, (i + 1) % count) for i in range(ends)])  13.7 us
    ppermute x4, starting transfers between devices, padded_2(): lax.ppermute(head, axis, [((i + 1) % count, i) for i in range(ends)])  11.2 us
    all_to_all x1, starting transfers between devices, per_device(): lax.all_to_all(jnp.stack(jnp.split(label_out, lax.axis_size('ev'), axis=1...  7.26 us
    all_to_all x1, starting transfers between devices, per_device(): lax.all_to_all(packed, 'ev', split_axis=1, concat_axis=1, tiled=True)  6.31 us
  transfers between devices with their start and end apart: 11, of which 11 were waited for; matrix products, arithmetic and copies ran while one was open for 2% of the time, Pallas kernels for 0%

profile of v1, /device:TPU:88, one launch (start us, length us, event | category | flops | bytes accessed | tf_op | source)
XLA Modules:
  0.0 172.3 jit_solution(16212414447941072230)
XLA Ops:
  0.0 0.8 fusion.47
  2.3 0.8 fusion.1
  8.0 7.3 %all-to-all-start = ((f32[8,1,2,1]{2,3,1,0:T(1,128)}), f32[8,1,2,1]{2,3,1,0:T(1,128)S(1)}, u32[]{:S(2)}, u32[]{:S(2)}) async-start(f32[8,1,2,1]{2,3,1,0:T(1,128)} %constant_dynamic-update-slice_fusion), calls=%async_computation | async-start | bytes 8192 | tf_op jit(solution)/shard_map/all_to_all | solution.py:54
  15.3 1.3 convolution_bitcast_fusion.1
  16.6 0.8 copy.44
  17.4 2.6 %all-to-all-done = f32[8,1,2,1]{2,3,1,0:T(1,128)S(1)} async-done(((f32[8,1,2,1]{2,3,1,0:T(1,128)}), f32[8,1,2,1]{2,3,1,0:T(1,128)S(1)}, u32[]{:S(2)}, u32[]{:S(2)}) %all-to-all-start) | async-done | bytes 96 | tf_op jit(solution)/shard_map/all_to_all | solution.py:54
  20.0 6.3 %all-to-all-start.1 = ((f32[32,16,128]{2,0,1:T(8,128)}), f32[32,16,128]{2,0,1:T(8,128)S(1)}, u32[]{:S(2)}, u32[]{:S(2)}) async-start(f32[32,16,128]{2,0,1:T(8,128)} %copy.44), calls=%async_computation.1 | async-start | bytes 524288 | tf_op jit(solution)/shard_map/all_to_all | solution.py:52
  27.6 4.5 %all-to-all-done.1 = f32[32,16,128]{2,0,1:T(8,128)S(1)} async-done(((f32[32,16,128]{2,0,1:T(8,128)}), f32[32,16,128]{2,0,1:T(8,128)S(1)}, u32[]{:S(2)}, u32[]{:S(2)}) %all-to-all-start.1) | async-done | bytes 262176 | tf_op jit(solution)/shard_map/all_to_all | solution.py:52
  33.0 1.0 convolution_bitcast_fusion
  34.0 1.0 copy.48
  35.0 16.2 %all-to-all-start.2 = ((f32[128,8,128]{2,1,0:T(8,128)}), f32[128,8,128]{2,1,0:T(8,128)S(1)}, u32[]{:S(2)}, u32[]{:S(2)}) async-start(f32[128,8,128]{2,1,0:T(8,128)} %copy.48), calls=%async_computation.2 | async-start | bytes 1048576 | tf_op jit(solution)/shard_map/all_to_all | solution.py:67
  51.3 29.4 %all-to-all-done.2 = f32[128,8,128]{2,1,0:T(8,128)S(1)} async-done(((f32[128,8,128]{2,1,0:T(8,128)}), f32[128,8,128]{2,1,0:T(8,128)S(1)}, u32[]{:S(2)}, u32[]{:S(2)}) %all-to-all-start.2) | async-done | bytes 524320 | tf_op jit(solution)/shard_map/all_to_all | solution.py:67
  80.9 5.4 %collective-permute-start.1 = (f32[2,512,1]{2,1,0:T(8,128)S(1)}, f32[2,512,1]{2,1,0:T(8,128)S(1)}, u32[]{:S(2)}, u32[]{:S(2)}) collective-permute-start(f32[2,512,1]{2,1,0:T(8,128)S(1)} %get-tuple-element.11), channel_id=1, source_target_pairs={{64,0},{128,64},{192,128},{256,192},{320,256},{384,320},{448,384},... | collective-permute-start | bytes 12296 | tf_op jit(solution)/shard_map/ppermute | solution.py:24
  86.3 1.9 %collective-permute-start = (f32[2,512,1]{2,1,0:T(8,128)S(1)}, f32[2,512,1]{2,1,0:T(8,128)S(1)}, u32[]{:S(2)}, u32[]{:S(2)}) collective-permute-start(f32[2,512,1]{2,1,0:T(8,128)S(1)} %get-tuple-element.12), channel_id=1, source_target_pairs={{0,64},{64,128},{128,192},{192,256},{256,320},{320,384},{384,448},... | collective-permute-start | bytes 12296 | tf_op jit(solution)/shard_map/ppermute | solution.py:22
  88.3 10.0 %collective-permute-done.1 = f32[2,512,1]{2,1,0:T(8,128)S(1)} collective-permute-done((f32[2,512,1]{2,1,0:T(8,128)S(1)}, f32[2,512,1]{2,1,0:T(8,128)S(1)}, u32[]{:S(2)}, u32[]{:S(2)}) %collective-permute-start.1) | collective-permute-done | bytes 4128 | tf_op jit(solution)/shard_map/ppermute | solution.py:24
  98.3 7.7 %collective-permute-done = f32[2,512,1]{2,1,0:T(8,128)S(1)} collective-permute-done((f32[2,512,1]{2,1,0:T(8,128)S(1)}, f32[2,512,1]{2,1,0:T(8,128)S(1)}, u32[]{:S(2)}, u32[]{:S(2)}) %collective-permute-start) | collective-permute-done | bytes 4128 | tf_op jit(solution)/shard_map/ppermute | solution.py:22
  106.5 0.8 fusion.3
  107.5 1.9 %collective-permute-start.3 = (f32[2,512,1]{2,1,0:T(8,128)S(1)}, f32[2,512,1]{2,1,0:T(8,128)S(1)}, u32[]{:S(2)}, u32[]{:S(2)}) collective-permute-start(f32[2,512,1]{2,1,0:T(8,128)S(1)} %get-tuple-element.9), channel_id=1, source_target_pairs={{64,0},{128,64},{192,128},{256,192},{320,256},{384,320},{448,384},... | collective-permute-start | bytes 12296 | tf_op jit(solution)/shard_map/ppermute | solution.py:24
  109.4 3.9 %collective-permute-start.2 = (f32[2,512,1]{2,1,0:T(8,128)S(1)}, f32[2,512,1]{2,1,0:T(8,128)S(1)}, u32[]{:S(2)}, u32[]{:S(2)}) collective-permute-start(f32[2,512,1]{2,1,0:T(8,128)S(1)} %get-tuple-element.10), channel_id=1, source_target_pairs={{0,64},{64,128},{128,192},{192,256},{256,320},{320,384},{384,448},... | collective-permute-start | bytes 12296 | tf_op jit(solution)/shard_map/ppermute | solution.py:22
  113.4 9.4 %collective-permute-done.3 = f32[2,512,1]{2,1,0:T(8,128)S(1)} collective-permute-done((f32[2,512,1]{2,1,0:T(8,128)S(1)}, f32[2,512,1]{2,1,0:T(8,128)S(1)}, u32[]{:S(2)}, u32[]{:S(2)}) %collective-permute-start.3) | collective-permute-done | bytes 4128 | tf_op jit(solution)/shard_map/ppermute | solution.py:24
  122.8 5.5 %collective-permute-done.2 = f32[2,512,1]{2,1,0:T(8,128)S(1)} collective-permute-done((f32[2,512,1]{2,1,0:T(8,128)S(1)}, f32[2,512,1]{2,1,0:T(8,128)S(1)}, u32[]{:S(2)}, u32[]{:S(2)}) %collective-permute-start.2) | collective-permute-done | bytes 4128 | tf_op jit(solution)/shard_map/ppermute | solution.py:22
  128.8 0.8 fusion.4
  129.8 1.9 %collective-permute-start.5 = (f32[2,512,1]{2,1,0:T(8,128)S(1)}, f32[2,512,1]{2,1,0:T(8,128)S(1)}, u32[]{:S(2)}, u32[]{:S(2)}) collective-permute-start(f32[2,512,1]{2,1,0:T(8,128)S(1)} %get-tuple-element.7), channel_id=1, source_target_pairs={{64,0},{128,64},{192,128},{256,192},{320,256},{384,320},{448,384},... | collective-permute-start | bytes 12296 | tf_op jit(solution)/shard_map/ppermute | solution.py:24
  131.7 3.9 %collective-permute-start.4 = (f32[2,512,1]{2,1,0:T(8,128)S(1)}, f32[2,512,1]{2,1,0:T(8,128)S(1)}, u32[]{:S(2)}, u32[]{:S(2)}) collective-permute-start(f32[2,512,1]{2,1,0:T(8,128)S(1)} %get-tuple-element.8), channel_id=1, source_target_pairs={{0,64},{64,128},{128,192},{192,256},{256,320},{320,384},{384,448},... | collective-permute-start | bytes 12296 | tf_op jit(solution)/shard_map/ppermute | solution.py:22
  135.6 8.6 %collective-permute-done.5 = f32[2,512,1]{2,1,0:T(8,128)S(1)} collective-permute-done((f32[2,512,1]{2,1,0:T(8,128)S(1)}, f32[2,512,1]{2,1,0:T(8,128)S(1)}, u32[]{:S(2)}, u32[]{:S(2)}) %collective-permute-start.5) | collective-permute-done | bytes 4128 | tf_op jit(solution)/shard_map/ppermute | solution.py:24
  144.2 5.5 %collective-permute-done.4 = f32[2,512,1]{2,1,0:T(8,128)S(1)} collective-permute-done((f32[2,512,1]{2,1,0:T(8,128)S(1)}, f32[2,512,1]{2,1,0:T(8,128)S(1)}, u32[]{:S(2)}, u32[]{:S(2)}) %collective-permute-start.4) | collective-permute-done | bytes 4128 | tf_op jit(solution)/shard_map/ppermute | solution.py:22
  150.2 0.8 fusion.5
  151.2 1.9 %collective-permute-start.7 = (f32[2,512,1]{2,1,0:T(8,128)S(1)}, f32[2,512,1]{2,1,0:T(8,128)S(1)}, u32[]{:S(2)}, u32[]{:S(2)}) collective-permute-start(f32[2,512,1]{2,1,0:T(8,128)S(1)} %get-tuple-element.5), channel_id=1, source_target_pairs={{64,0},{128,64},{192,128},{256,192},{320,256},{384,320},{448,384},... | collective-permute-start | bytes 12296 | tf_op jit(solution)/shard_map/ppermute | solution.py:24
  153.1 3.9 %collective-permute-start.6 = (f32[2,512,1]{2,1,0:T(8,128)S(1)}, f32[2,512,1]{2,1,0:T(8,128)S(1)}, u32[]{:S(2)}, u32[]{:S(2)}) collective-permute-start(f32[2,512,1]{2,1,0:T(8,128)S(1)} %get-tuple-element.6), channel_id=1, source_target_pairs={{0,64},{64,128},{128,192},{192,256},{256,320},{320,384},{384,448},... | collective-permute-start | bytes 12296 | tf_op jit(solution)/shard_map/ppermute | solution.py:22
  157.1 7.7 %collective-permute-done.7 = f32[2,512,1]{2,1,0:T(8,128)S(1)} collective-permute-done((f32[2,512,1]{2,1,0:T(8,128)S(1)}, f32[2,512,1]{2,1,0:T(8,128)S(1)}, u32[]{:S(2)}, u32[]{:S(2)}) %collective-permute-start.7) | collective-permute-done | bytes 4128 | tf_op jit(solution)/shard_map/ppermute | solution.py:24
  164.8 5.5 %collective-permute-done.6 = f32[2,512,1]{2,1,0:T(8,128)S(1)} collective-permute-done((f32[2,512,1]{2,1,0:T(8,128)S(1)}, f32[2,512,1]{2,1,0:T(8,128)S(1)}, u32[]{:S(2)}, u32[]{:S(2)}) %collective-permute-start.6) | collective-permute-done | bytes 4128 | tf_op jit(solution)/shard_map/ppermute | solution.py:22
  170.8 1.5 fusion.6
  (33 shorter events, 11.3 us)
Async XLA Ops:
  0.0 88.2 %copy-start = (f32[512,1024]{1,0:T(8,128)S(1)}, f32[512,1024]{1,0:T(8,128)}, u32[]{:S(2)}) copy-start(f32[512,1024]{1,0:T(8,128)} %param.9) | copy-start | bytes 6291460
  8.0 12.0 %all-to-all-start = ((f32[8,1,2,1]{2,3,1,0:T(1,128)}), f32[8,1,2,1]{2,3,1,0:T(1,128)S(1)}, u32[]{:S(2)}, u32[]{:S(2)}) async-start(f32[8,1,2,1]{2,3,1,0:T(1,128)} %constant_dynamic-update-slice_fusion), calls=%async_computation | async-start | bytes 8192 | tf_op jit(solution)/shard_map/all_to_all | solution.py:54
  17.4 15.6 %copy-start.1 = (f32[128,128]{1,0:T(8,128)S(1)}, f32[128,128]{1,0:T(8,128)}, u32[]{:S(2)}) copy-start(f32[128,128]{1,0:T(8,128)} %param.7) | copy-start | bytes 196612
  20.0 12.1 %all-to-all-start.1 = ((f32[32,16,128]{2,0,1:T(8,128)}), f32[32,16,128]{2,0,1:T(8,128)S(1)}, u32[]{:S(2)}, u32[]{:S(2)}) async-start(f32[32,16,128]{2,0,1:T(8,128)} %copy.44), calls=%async_computation.1 | async-start | bytes 524288 | tf_op jit(solution)/shard_map/all_to_all | solution.py:52
  34.0 17.2 %copy-start.2 = (s32[2]{0:T(128)S(1)}, s32[2]{0:T(128)}, u32[]{:S(2)}) copy-start(s32[2]{0:T(128)} %param.8) | copy-start | bytes 28
  35.0 45.6 %all-to-all-start.2 = ((f32[128,8,128]{2,1,0:T(8,128)}), f32[128,8,128]{2,1,0:T(8,128)S(1)}, u32[]{:S(2)}, u32[]{:S(2)}) async-start(f32[128,8,128]{2,1,0:T(8,128)} %copy.48), calls=%async_computation.2 | async-start | bytes 1048576 | tf_op jit(solution)/shard_map/all_to_all | solution.py:67
  80.9 17.4 %collective-permute-start.1 = (f32[2,512,1]{2,1,0:T(8,128)S(1)}, f32[2,512,1]{2,1,0:T(8,128)S(1)}, u32[]{:S(2)}, u32[]{:S(2)}) collective-permute-start(f32[2,512,1]{2,1,0:T(8,128)S(1)} %get-tuple-element.11), channel_id=1, source_target_pairs={{64,0},{128,64},{192,128},{256,192},{320,256},{384,320},{448,384},... | collective-permute-start | bytes 12296 | tf_op jit(solution)/shard_map/ppermute | solution.py:24
  86.3 19.7 %collective-permute-start = (f32[2,512,1]{2,1,0:T(8,128)S(1)}, f32[2,512,1]{2,1,0:T(8,128)S(1)}, u32[]{:S(2)}, u32[]{:S(2)}) collective-permute-start(f32[2,512,1]{2,1,0:T(8,128)S(1)} %get-tuple-element.12), channel_id=1, source_target_pairs={{0,64},{64,128},{128,192},{192,256},{256,320},{320,384},{384,448},... | collective-permute-start | bytes 12296 | tf_op jit(solution)/shard_map/ppermute | solution.py:22
  107.5 15.3 %collective-permute-start.3 = (f32[2,512,1]{2,1,0:T(8,128)S(1)}, f32[2,512,1]{2,1,0:T(8,128)S(1)}, u32[]{:S(2)}, u32[]{:S(2)}) collective-permute-start(f32[2,512,1]{2,1,0:T(8,128)S(1)} %get-tuple-element.9), channel_id=1, source_target_pairs={{64,0},{128,64},{192,128},{256,192},{320,256},{384,320},{448,384},... | collective-permute-start | bytes 12296 | tf_op jit(solution)/shard_map/ppermute | solution.py:24
  109.4 18.9 %collective-permute-start.2 = (f32[2,512,1]{2,1,0:T(8,128)S(1)}, f32[2,512,1]{2,1,0:T(8,128)S(1)}, u32[]{:S(2)}, u32[]{:S(2)}) collective-permute-start(f32[2,512,1]{2,1,0:T(8,128)S(1)} %get-tuple-element.10), channel_id=1, source_target_pairs={{0,64},{64,128},{128,192},{192,256},{256,320},{320,384},{384,448},... | collective-permute-start | bytes 12296 | tf_op jit(solution)/shard_map/ppermute | solution.py:22
  129.8 14.4 %collective-permute-start.5 = (f32[2,512,1]{2,1,0:T(8,128)S(1)}, f32[2,512,1]{2,1,0:T(8,128)S(1)}, u32[]{:S(2)}, u32[]{:S(2)}) collective-permute-start(f32[2,512,1]{2,1,0:T(8,128)S(1)} %get-tuple-element.7), channel_id=1, source_target_pairs={{64,0},{128,64},{192,128},{256,192},{320,256},{384,320},{448,384},... | collective-permute-start | bytes 12296 | tf_op jit(solution)/shard_map/ppermute | solution.py:24
  131.7 18.0 %collective-permute-start.4 = (f32[2,512,1]{2,1,0:T(8,128)S(1)}, f32[2,512,1]{2,1,0:T(8,128)S(1)}, u32[]{:S(2)}, u32[]{:S(2)}) collective-permute-start(f32[2,512,1]{2,1,0:T(8,128)S(1)} %get-tuple-element.8), channel_id=1, source_target_pairs={{0,64},{64,128},{128,192},{192,256},{256,320},{320,384},{384,448},... | collective-permute-start | bytes 12296 | tf_op jit(solution)/shard_map/ppermute | solution.py:22
  151.2 13.6 %collective-permute-start.7 = (f32[2,512,1]{2,1,0:T(8,128)S(1)}, f32[2,512,1]{2,1,0:T(8,128)S(1)}, u32[]{:S(2)}, u32[]{:S(2)}) collective-permute-start(f32[2,512,1]{2,1,0:T(8,128)S(1)} %get-tuple-element.5), channel_id=1, source_target_pairs={{64,0},{128,64},{192,128},{256,192},{320,256},{384,320},{448,384},... | collective-permute-start | bytes 12296 | tf_op jit(solution)/shard_map/ppermute | solution.py:24
  153.1 17.2 %collective-permute-start.6 = (f32[2,512,1]{2,1,0:T(8,128)S(1)}, f32[2,512,1]{2,1,0:T(8,128)S(1)}, u32[]{:S(2)}, u32[]{:S(2)}) collective-permute-start(f32[2,512,1]{2,1,0:T(8,128)S(1)} %get-tuple-element.6), channel_id=1, source_target_pairs={{0,64},{64,128},{128,192},{192,256},{256,320},{320,384},{384,448},... | collective-permute-start | bytes 12296 | tf_op jit(solution)/shard_map/ppermute | solution.py:22
